TPU v7x, 256 devices: a whole 4x4x8 slice. The times are simulated.
256 devices in a mesh: section: 8 (over y, x_hi), ctx: 32 (over x_lo, z, core).
Axes of the slice: x: 4 (x_hi: 2, x_lo: 2; x = x_hi * 2 + x_lo), y: 4, z: 8, core: 2. Of those that a mesh axis runs over, the one named last changes fastest.
Arguments:
- latent_state: bfloat16 [8, 5120, 1536], P('section', 'ctx'), may hold values from -20 to 20
- lead_step: int32 [8], replicated, may hold values from 0 to 7, each once
- tail_qkv: bfloat16 [1536, 1280], P(('section', 'ctx')), may hold values from -0.15625 to 0.15625
- tail_out: bfloat16 [1536, 768], P(('section', 'ctx')), may hold values from -0.21875 to 0.21875
- head_qkv: bfloat16 [1536, 1280], P(('section', 'ctx')), may hold values from -0.15625 to 0.15625
- head_out: bfloat16 [1536, 768], P(('section', 'ctx')), may hold values from -0.21875 to 0.21875
- modulation: float32 [2, 2, 9, 1536], replicated, may hold values from 0.5 to 1.5
- qk_gain: float32 [2, 2, 128], replicated, may hold values from 1 to 2
Outputs:
- tail_state: bfloat16 [8, 5120, 1536], P('section', 'ctx')
- head_state: bfloat16 [8, 5120, 1536], P('section', 'ctx')
Inputs may be any that keep to these rules, and one draw needn't show every extreme that they name: `lead_step`: every section holds a different lead time.
All inputs are finite; a program needn't handle non-finite values.
Results may differ from a plain program's by a relative error of at most 0.01.
Values may be sent and summed in bfloat16 or wider, within the bound.
No kernel may reach another device: no remote copies, remote signals or barrier semaphores. Data moves between devices by JAX's collectives and lax.ppermute only.
A program may use at most 64 MiB of HBM per device.

v0:
```python
import jax
import jax.numpy as jnp
from jax import lax
from jax.sharding import PartitionSpec as P

QH = 6
KVH = 2
HD = 128


def passed_along(x, axis, by):
    peers = lax.axis_size(axis)
    return lax.ppermute(x, axis, [(i, (i + by) % peers) for i in range(peers)])


def qk_normal(values, gain_row):
    factor = lax.rsqrt(jnp.mean(values * values, axis=-1, keepdims=True) + 1e-06)
    return (values * factor * gain_row).astype(jnp.bfloat16)


def fetch_weights(joined_w, output_w):
    return (
        lax.all_gather(joined_w, ("section", "ctx"), axis=0, tiled=True),
        lax.all_gather(output_w, ("section", "ctx"), axis=0, tiled=True),
    )


def attend(inputs, joined_w, output_w, gain_rows, q_gain, k_gain):
    tok_rows = inputs.shape[0]
    groups = QH // KVH
    q_width = QH * HD
    k_width = KVH * HD
    score_scale = float(HD) ** (-0.5)
    widened = inputs.astype(jnp.float32)
    factor = lax.rsqrt(jnp.mean(widened * widened, axis=-1, keepdims=True) + 1e-06)
    normed = (widened * factor * gain_rows[0]).astype(jnp.bfloat16)
    projected = jnp.dot(normed, joined_w, preferred_element_type=jnp.float32)
    queries = qk_normal(projected[:, :q_width].reshape(tok_rows, KVH, groups, HD), q_gain)
    key_rows = qk_normal(
        projected[:, q_width : q_width + k_width].reshape(tok_rows, KVH, HD), k_gain
    )
    key_rows = key_rows.reshape(tok_rows, k_width)
    val_rows = projected[:, q_width + k_width :].astype(jnp.bfloat16)

    def add_block(running, key_block, val_block):
        scores = (
            jnp.einsum("tkgd,skd->tkgs", queries, key_block, preferred_element_type=jnp.float32)
            * score_scale
        )
        weights = jnp.exp(scores)
        numerator = running[0] + jnp.einsum(
            "tkgs,skd->tkgd",
            weights.astype(jnp.bfloat16),
            val_block,
            preferred_element_type=jnp.float32,
        )
        return (numerator, running[1] + jnp.sum(weights, axis=-1))

    initial = (
        jnp.zeros((tok_rows, KVH, groups, HD), jnp.float32),
        jnp.zeros((tok_rows, KVH, groups), jnp.float32),
    )
    running = initial
    pieces = (
        lax.all_gather(key_rows, "ctx", axis=0, tiled=True),
        lax.all_gather(val_rows, "ctx", axis=0, tiled=True),
    )
    row_count = pieces[0].shape[0]
    key_piece = pieces[0].reshape(row_count, KVH, HD)
    val_piece = pieces[1].reshape(row_count, KVH, HD)
    key_blocks = key_piece.reshape(row_count // 256, 256, KVH, HD)
    val_blocks = val_piece.reshape(row_count // 256, 256, KVH, HD)

    def step_block(state_pair, block_pair):
        return (add_block(state_pair, block_pair[0], block_pair[1]), None)

    running, unused = lax.scan(step_block, running, (key_blocks, val_blocks))
    numerator, denominator = running
    attended = (numerator / denominator[..., None]).astype(jnp.bfloat16).reshape(tok_rows, q_width)
    update = lax.dot_general(
        attended, output_w, (((1,), (1,)), ((), ())), preferred_element_type=jnp.float32
    )
    return (widened + gain_rows[1] * update).astype(jnp.bfloat16)


def per_device(
    latent_state, lead_step, tail_qkv, tail_out, head_qkv, head_out, modulation, qk_gain
):
    section_pos = lax.axis_index("section")
    section_count = lax.axis_size("section")
    lead_now = lax.dynamic_index_in_dim(lead_step, section_pos, 0, keepdims=False)
    sender = jnp.mod(section_pos - 1 + section_count, section_count)
    lead_next = lax.dynamic_index_in_dim(lead_step, sender, 0, keepdims=False) + 1
    tail_rows = lax.dynamic_index_in_dim(modulation[0], lead_now, 1, keepdims=False)
    head_rows = lax.dynamic_index_in_dim(modulation[1], lead_next, 1, keepdims=False)
    tail_weights = fetch_weights(tail_qkv, tail_out)
    tail_new = attend(
        latent_state[0], tail_weights[0], tail_weights[1], tail_rows, qk_gain[0, 0], qk_gain[0, 1]
    )
    arrived = passed_along(tail_new, "section", 1)
    head_weights = fetch_weights(head_qkv, head_out)
    head_new = attend(
        arrived, head_weights[0], head_weights[1], head_rows, qk_gain[1, 0], qk_gain[1, 1]
    )
    return (tail_new[None], head_new[None])


def solution(mesh):
    in_specs = (
        P("section", "ctx", None),
        P(),
        P(("section", "ctx"), None),
        P(("section", "ctx"), None),
        P(("section", "ctx"), None),
        P(("section", "ctx"), None),
        P(),
        P(),
    )
    out_specs = (P("section", "ctx", None), P("section", "ctx", None))
    return jax.shard_map(
        per_device, mesh=mesh, in_specs=in_specs, out_specs=out_specs, check_vma=False
    )
```

profile of v0, /device:TPU:1, one launch (start us, length us, event | category | flops | bytes accessed | tf_op | source)
XLA Modules:
  0.0 803.6 jit_solution(7002405267562362757)
XLA Ops:
  12.0 1.6 fusion.34
  15.6 115.7 %all-gather.21.cloned.1.call-done = bf16[256,6,1280]{2,1,0:T(8,128)(2,1)} async-done(((bf16[1,6,1280]{2,1,0:T(8,128)(2,1)}), bf16[256,6,1280]{2,1,0:T(8,128)(2,1)}) %all-gather.21.cloned.1.call-update) | async-done | bytes 3932176 | tf_op jit(solution)/shard_map/all_gather | solution.py:23
  131.4 7.3 reshape.102
  138.6 3.0 fusion.19
  144.9 92.6 %all-gather.23.cloned.1.call-done = bf16[256,6,768]{2,1,0:T(8,128)(2,1)} async-done(((bf16[1,6,768]{2,1,0:T(8,128)(2,1)}), bf16[256,6,768]{2,1,0:T(8,128)(2,1)}) %all-gather.23.cloned.1.call-update) | async-done | bytes 2359312 | tf_op jit(solution)/shard_map/all_gather | solution.py:24
  237.5 3.8 reshape.104
  241.3 1.8 slice.72
  249.6 54.2 %all-gather.15.cloned.1.call-done = bf16[5120,256]{1,0:T(8,128)(2,1)} async-done(((bf16[160,256]{1,0:T(8,128)(2,1)}), bf16[5120,256]{1,0:T(8,128)(2,1)}) %all-gather.15.cloned.1.call-update) | async-done | bytes 2621456 | tf_op jit(solution)/shard_map/all_gather | solution.py:65
  303.8 4.9 reshape_reshape.13
  308.7 62.7 %all-gather.13.cloned.1.call-done = bf16[5120,256]{1,0:T(8,128)(2,1)} async-done(((bf16[160,256]{1,0:T(8,128)(2,1)}), bf16[5120,256]{1,0:T(8,128)(2,1)}) %all-gather.13.cloned.1.call-update) | async-done | bytes 2621456 | tf_op jit(solution)/shard_map/all_gather | solution.py:66
  371.4 4.9 reshape_reshape.12
  376.3 59.0 %while.26 = (s32[]{:T(128)}, f32[160,2,3,128]{3,0,2,1:T(8,128)S(1)}, f32[160,2,3]{0,2,1:T(4,128)S(1)}, bf16[20,256,2,128]{3,2,1,0:T(2,128)(2,1)}, bf16[20,256,2,...) while((s32[]{:T(128)}, f32[160,2,3,128]{3,0,2,1:T(8,128)S(1)}, ...), condition=%wide.region_5.6_spmd.clone, body=%wide.region_3.5_spmd.clone.sunk | while | flops 126813120 | bytes 3013732 | solution.py:77
  377.4 1.4 fusion.56
  383.3 1.4 fusion.56
  386.3 1.4 fusion.56
  389.2 1.4 fusion.56
  392.2 1.4 fusion.56
  395.1 1.4 fusion.56
  398.1 1.4 fusion.56
  401.0 1.4 fusion.56
  404.0 1.4 fusion.56
  412.8 1.4 fusion.56
  421.7 1.4 fusion.56
  430.5 1.4 fusion.56
  435.9 1.9 fusion.11
  437.8 2.5 collective-permute-start
  442.5 47.7 %all-gather.25.cloned.1.call-done = bf16[256,6,1280]{2,1,0:T(8,128)(2,1)} async-done(((bf16[1,6,1280]{2,1,0:T(8,128)(2,1)}), bf16[256,6,1280]{2,1,0:T(8,128)(2,1)}) %all-gather.25.cloned.1.call-update) | async-done | bytes 3932176 | tf_op jit(solution)/shard_map/all_gather | solution.py:23
  490.1 7.2 reshape.106
  497.6 3.0 fusion.21
  502.8 93.4 %all-gather.27.cloned.1.call-done = bf16[256,6,768]{2,1,0:T(8,128)(2,1)} async-done(((bf16[1,6,768]{2,1,0:T(8,128)(2,1)}), bf16[256,6,768]{2,1,0:T(8,128)(2,1)}) %all-gather.27.cloned.1.call-update) | async-done | bytes 2359312 | tf_op jit(solution)/shard_map/all_gather | solution.py:24
  596.2 3.8 reshape.108
  599.9 1.8 slice.75
  608.2 54.2 %all-gather.19.cloned.1.call-done = bf16[5120,256]{1,0:T(8,128)(2,1)} async-done(((bf16[160,256]{1,0:T(8,128)(2,1)}), bf16[5120,256]{1,0:T(8,128)(2,1)}) %all-gather.19.cloned.1.call-update) | async-done | bytes 2621456 | tf_op jit(solution)/shard_map/all_gather | solution.py:65
  662.4 4.9 reshape_reshape.15
  667.3 62.2 %all-gather.17.cloned.1.call-done = bf16[5120,256]{1,0:T(8,128)(2,1)} async-done(((bf16[160,256]{1,0:T(8,128)(2,1)}), bf16[5120,256]{1,0:T(8,128)(2,1)}) %all-gather.17.cloned.1.call-update) | async-done | bytes 2621456 | tf_op jit(solution)/shard_map/all_gather | solution.py:66
  729.6 4.9 reshape_reshape.14
  734.5 58.9 %while.27 = (s32[]{:T(128)}, f32[160,2,3,128]{3,0,2,1:T(8,128)S(1)}, f32[160,2,3]{0,2,1:T(4,128)S(1)}, bf16[20,256,2,128]{3,2,1,0:T(2,128)(2,1)}, bf16[20,256,2,...) while((s32[]{:T(128)}, ...), condition=%wide.region_11.12_spmd.clone, body=%wide.region_9.11_spmd.clone.sunk | while | flops 126813120 | bytes 3013732 | solution.py:77
  741.5 1.4 fusion.60
  744.5 1.4 fusion.60
  747.4 1.4 fusion.60
  750.3 1.4 fusion.60
  753.3 1.4 fusion.60
  756.2 1.4 fusion.60
  759.2 1.4 fusion.60
  762.1 1.4 fusion.60
  776.9 1.4 fusion.60
  782.8 1.4 fusion.60
  794.0 2.7 fusion.12
  (213 shorter events, 110.6 us)
Async XLA Ops:
  7.2 124.2 %all-gather.21.cloned.1.call-start = ((), (), s32[]{:S(2)}) async-start(), calls=%async_computation.4 | async-start | bytes 5263360 | tf_op jit(solution)/shard_map/all_gather | solution.py:23
  7.9 229.6 %all-gather.23.cloned.1.call-start = ((), (), s32[]{:S(2)}) async-start(), calls=%async_computation.5 | async-start | bytes 3158016 | tf_op jit(solution)/shard_map/all_gather | solution.py:24
  8.6 295.2 %all-gather.15.cloned.1.call-start = ((), (), s32[]{:S(2)}) async-start(), calls=%async_computation.1 | async-start | bytes 2703360 | tf_op jit(solution)/shard_map/all_gather | solution.py:65
  15.6 123.0 %copy-start = (bf16[1,160,1536]{2,1,0:T(8,128)(2,1)S(1)}, bf16[1,160,1536]{2,1,0:T(8,128)(2,1)}, u32[]{:S(2)}) copy-start(bf16[1,160,1536]{2,1,0:T(8,128)(2,1)} %param.12) | copy-start | bytes 1474564
  141.6 3.3 copy-start.2
  142.9 228.4 %all-gather.13.cloned.1.call-start = ((), (), s32[]{:S(2)}) async-start(), calls=%async_computation | async-start | bytes 2703360 | tf_op jit(solution)/shard_map/all_gather | solution.py:66
  143.6 346.5 %all-gather.25.cloned.1.call-start = ((), (), s32[]{:S(2)}) async-start(), calls=%async_computation.6 | async-start | bytes 5263360 | tf_op jit(solution)/shard_map/all_gather | solution.py:23
  144.2 451.9 %all-gather.27.cloned.1.call-start = ((), (), s32[]{:S(2)}) async-start(), calls=%async_computation.7 | async-start | bytes 3158016 | tf_op jit(solution)/shard_map/all_gather | solution.py:24
  144.8 517.6 %all-gather.19.cloned.1.call-start = ((), (), s32[]{:S(2)}) async-start(), calls=%async_computation.3 | async-start | bytes 2703360 | tf_op jit(solution)/shard_map/all_gather | solution.py:65
  437.8 59.5 %copy-start.4 = (bf16[160,1536]{1,0:T(8,128)(2,1)}, bf16[160,1536]{1,0:T(8,128)(2,1)S(1)}, u32[]{:S(2)}) copy-start(bf16[160,1536]{1,0:T(8,128)(2,1)S(1)} %fusion.11) | copy-start | bytes 1474564
  437.8 59.5 %collective-permute-start = (bf16[160,1536]{1,0:T(8,128)(2,1)S(1)}, bf16[160,1536]{1,0:T(8,128)(2,1)S(1)}, u32[]{:S(2)}, u32[]{:S(2)}) collective-permute-start(bf16[160,1536]{1,0:T(8,128)(2,1)S(1)} %fusion.11), channel_id=1, source_target_pairs={{0,32},{32,64},{64,96},{96,128},{128,160},{160,192},{192,224},{224... | collective-permute-start | bytes 1474568 | tf_op jit(solution)/shard_map/ppermute | solution.py:13
  497.4 3.2 copy-start.1
  500.6 2.2 copy-start.3
  501.9 227.7 %all-gather.17.cloned.1.call-start = ((), (), s32[]{:S(2)}) async-start(), calls=%async_computation.2 | async-start | bytes 2703360 | tf_op jit(solution)/shard_map/all_gather | solution.py:66
Sparse Core Ops, SparseCore 0:
  11.6 119.7 all-gather.20
  134.9 102.5 all-gather.22
  239.4 64.3 all-gather.14
  306.1 65.2 all-gather.12
  374.8 115.3 all-gather.24
  493.5 102.5 all-gather.26
  598.0 64.3 all-gather.18
  664.3 65.2 all-gather.16
where the time goes:
time: 807 us; the launch traced here: 804 us
  waiting for transfers between devices  585 us (72%)
  local copies, waits for them, and re-layouts  106 us (13%)
  matrix products  80.5 us (10%)
  between operations  17.7 us (2%)
  other arithmetic  9.34 us (1%)
    all_gather x2, waiting for transfers between devices, fetch_weights(): lax.all_gather(output_w, ('section', 'ctx'), axis=0, tiled=True)  186 us
    all_gather x2, waiting for transfers between devices, fetch_weights(): lax.all_gather(joined_w, ('section', 'ctx'), axis=0, tiled=True)  163 us
    all_gather x2, waiting for transfers between devices, attend(): lax.all_gather(val_rows, 'ctx', axis=0, tiled=True)  125 us
    all_gather x2, waiting for transfers between devices, attend(): lax.all_gather(key_rows, 'ctx', axis=0, tiled=True)  108 us
    dot_general x40, matrix products, add_block(): jnp.einsum('tkgd,skd->tkgs', queries, key_block, preferred_element_type=j...  56.5 us
    dynamic_slice x40, local copies, waits for them, and re-layouts, attend(): running, unused = lax.scan(step_block, running, (key_blocks, val_blocks))  46.1 us
    unnamed x16, local copies, waits for them, and re-layouts  23.5 us
  transfers between devices with their start and end apart: 9, of which 8 were waited for; matrix products, arithmetic and copies ran while one was open for 16% of the time, Pallas kernels for 0%

commit v1 on v0

--- a/solution.py
+++ b/solution.py
@@ -21,7 +21,12 @@
 def fetch_weights(joined_w, output_w):
     return (
         lax.all_gather(joined_w, ("section", "ctx"), axis=0, tiled=True),
-        lax.all_gather(output_w, ("section", "ctx"), axis=0, tiled=True),
+        jnp.concatenate(
+            lax.all_to_all(
+                jnp.stack([output_w] * lax.axis_size(("section", "ctx"))), ("section", "ctx"), 0, 0
+            ),
+            axis=0,
+        ),
     )
 
 

time: 807 us -> 638 us (0.79)
  waiting for transfers between devices: 585 us -> 393 us
  starting transfers between devices: 2.99 us -> 22.4 us
    all_gather x2 -> x0, waiting for transfers between devices: 186 us -> none  [fetch_weights(): lax.all_gather(output_w, ('section', 'ctx'), axis=0, tiled=True)]
    all_to_all x0 -> x2, waiting for transfers between devices: none -> 177 us  [fetch_weights(): lax.all_to_all(jnp.stack([output_w] * lax.axis_size(('section', 'ctx'))),...]
    all_gather x2, waiting for transfers between devices: 108 us -> 0.01 us  [attend(): lax.all_gather(key_rows, 'ctx', axis=0, tiled=True)]
    all_gather x2, waiting for transfers between devices: 125 us -> 50.1 us  [attend(): lax.all_gather(val_rows, 'ctx', axis=0, tiled=True)]
    all_to_all x0 -> x2, starting transfers between devices: none -> 19.2 us  [fetch_weights(): lax.all_to_all(jnp.stack([output_w] * lax.axis_size(('section', 'ctx'))),...]
    unnamed x16 -> x18, local copies, waits for them, and re-layouts: 23.5 us -> 16.1 us
  transfers between devices with their start and end apart: 9 -> 9, of which waited for: 8 -> 6; matrix products, arithmetic and copies ran while one was open for 16% -> 19% of each run, Pallas kernels for 0% -> 0%
where the time goes in v1:
time: 638 us; the launch traced here: 634 us
  waiting for transfers between devices  393 us (62%)
  local copies, waits for them, and re-layouts  110 us (17%)
  matrix products  80.5 us (13%)
  starting transfers between devices  22.4 us (4%)
  between operations  17.8 us (3%)
  other arithmetic  9.32 us (1%)
    all_to_all x2, waiting for transfers between devices, fetch_weights(): lax.all_to_all(jnp.stack([output_w] * lax.axis_size(('section', 'ctx'))),...  177 us
    all_gather x2, waiting for transfers between devices, fetch_weights(): lax.all_gather(joined_w, ('section', 'ctx'), axis=0, tiled=True)  164 us
    dot_general x40, matrix products, add_block(): jnp.einsum('tkgd,skd->tkgs', queries, key_block, preferred_element_type=j...  56.5 us
    all_gather x2, waiting for transfers between devices, attend(): lax.all_gather(val_rows, 'ctx', axis=0, tiled=True)  50.1 us
    dynamic_slice x40, local copies, waits for them, and re-layouts, attend(): running, unused = lax.scan(step_block, running, (key_blocks, val_blocks))  46.1 us
    all_to_all x2, starting transfers between devices, fetch_weights(): lax.all_to_all(jnp.stack([output_w] * lax.axis_size(('section', 'ctx'))),...  19.2 us
    unnamed x18, local copies, waits for them, and re-layouts  16.1 us
    dot_general x40, matrix products, add_block(): jnp.einsum('tkgs,skd->tkgd', weights.astype(jnp.bfloat16), val_block, pre...  13.3 us
  transfers between devices with their start and end apart: 9, of which 6 were waited for; matrix products, arithmetic and copies ran while one was open for 19% of the time, Pallas kernels for 0%

profile of v1, /device:TPU:1, one launch (start us, length us, event | category | flops | bytes accessed | tf_op | source)
XLA Modules:
  0.0 634.4 jit_solution(18444111928200730918)
XLA Ops:
  11.3 1.6 fusion.34
  14.9 116.4 %all-gather.17.cloned.1.call-done = bf16[256,6,1280]{2,1,0:T(8,128)(2,1)} async-done(((bf16[1,6,1280]{2,1,0:T(8,128)(2,1)}), bf16[256,6,1280]{2,1,0:T(8,128)(2,1)}) %all-gather.17.cloned.1.call-update) | async-done | bytes 3932176 | tf_op jit(solution)/shard_map/all_gather | solution.py:23
  131.4 7.3 %reshape.114 = bf16[1536,1280]{1,0:T(8,128)(2,1)} reshape(bf16[256,6,1280]{2,1,0:T(8,128)(2,1)} %all-gather.17.cloned.1.call-done) | data formatting | bytes 7864320
  138.6 3.0 fusion.19
  143.7 1.9 stack.4
  145.6 9.6 %all-to-all-start = ((bf16[256,6,768]{2,1,0:T(8,128)(2,1)}), bf16[256,6,768]{2,1,0:T(8,128)(2,1)}, u32[]{:S(2)}, u32[]{:S(2)}) async-start(bf16[256,6,768]{2,1,0:T(8,128)(2,1)} %stack.4), calls=%async_computation | async-start | bytes 6291456 | tf_op jit(solution)/shard_map/all_to_all | solution.py:25
  155.8 88.1 %all-to-all-done = bf16[256,6,768]{2,1,0:T(8,128)(2,1)} async-done(((bf16[256,6,768]{2,1,0:T(8,128)(2,1)}), bf16[256,6,768]{2,1,0:T(8,128)(2,1)}, u32[]{:S(2)}, u32[]{:S(2)}) %all-to-all-start) | async-done | bytes 2359328 | tf_op jit(solution)/shard_map/all_to_all | solution.py:25
  244.0 3.8 reshape.108
  247.8 1.8 slice.72
  256.0 4.9 reshape_reshape.13
  260.9 25.8 %all-gather.9.cloned.1.call-done = bf16[5120,256]{1,0:T(8,128)(2,1)} async-done(((bf16[160,256]{1,0:T(8,128)(2,1)}), bf16[5120,256]{1,0:T(8,128)(2,1)}) %all-gather.9.cloned.1.call-update) | async-done | bytes 2621456 | tf_op jit(solution)/shard_map/all_gather | solution.py:71
  286.8 4.9 reshape_reshape.12
  291.7 59.0 %while.26 = (s32[]{:T(128)}, f32[160,2,3,128]{3,0,2,1:T(8,128)S(1)}, f32[160,2,3]{0,2,1:T(4,128)S(1)}, bf16[20,256,2,128]{3,2,1,0:T(2,128)(2,1)}, bf16[20,256,2,...) while((s32[]{:T(128)}, f32[160,2,3,128]{3,0,2,1:T(8,128)S(1)}, ...), condition=%wide.region_5.6_spmd.clone, body=%wide.region_3.5_spmd.clone.sunk | while | flops 126813120 | bytes 3013732 | solution.py:82
  292.8 1.4 fusion.56
  295.8 1.4 fusion.56
  301.7 1.4 fusion.56
  304.6 1.4 fusion.56
  313.5 1.4 fusion.56
  316.4 1.4 fusion.56
  319.4 1.4 fusion.56
  322.3 1.4 fusion.56
  325.3 1.4 fusion.56
  328.2 1.4 fusion.56
  334.1 1.4 fusion.56
  337.1 1.4 fusion.56
  340.0 1.4 fusion.56
  348.9 1.4 fusion.56
  351.2 1.9 fusion.11
  353.2 2.9 collective-permute-start
  358.3 47.5 %all-gather.19.cloned.1.call-done = bf16[256,6,1280]{2,1,0:T(8,128)(2,1)} async-done(((bf16[1,6,1280]{2,1,0:T(8,128)(2,1)}), bf16[256,6,1280]{2,1,0:T(8,128)(2,1)}) %all-gather.19.cloned.1.call-update) | async-done | bytes 3932176 | tf_op jit(solution)/shard_map/all_gather | solution.py:23
  405.8 7.3 %reshape.116 = bf16[1536,1280]{1,0:T(8,128)(2,1)} reshape(bf16[256,6,1280]{2,1,0:T(8,128)(2,1)} %all-gather.19.cloned.1.call-done) | data formatting | bytes 7864320
  413.3 3.0 fusion.21
  417.6 1.9 stack.5
  419.5 9.6 %all-to-all-start.1 = ((bf16[256,6,768]{2,1,0:T(8,128)(2,1)}), bf16[256,6,768]{2,1,0:T(8,128)(2,1)}, u32[]{:S(2)}, u32[]{:S(2)}) async-start(bf16[256,6,768]{2,1,0:T(8,128)(2,1)} %stack.5), calls=%async_computation.1 | async-start | bytes 6291456 | tf_op jit(solution)/shard_map/all_to_all | solution.py:25
  430.0 89.1 %all-to-all-done.1 = bf16[256,6,768]{2,1,0:T(8,128)(2,1)} async-done(((bf16[256,6,768]{2,1,0:T(8,128)(2,1)}), bf16[256,6,768]{2,1,0:T(8,128)(2,1)}, u32[]{:S(2)}, u32[]{:S(2)}) %all-to-all-start.1) | async-done | bytes 2359328 | tf_op jit(solution)/shard_map/all_to_all | solution.py:25
  519.1 3.8 reshape.111
  522.9 1.8 slice.75
  531.2 4.9 reshape_reshape.15
  536.1 24.3 %all-gather.13.cloned.1.call-done = bf16[5120,256]{1,0:T(8,128)(2,1)} async-done(((bf16[160,256]{1,0:T(8,128)(2,1)}), bf16[5120,256]{1,0:T(8,128)(2,1)}) %all-gather.13.cloned.1.call-update) | async-done | bytes 2621456 | tf_op jit(solution)/shard_map/all_gather | solution.py:71
  560.4 4.9 reshape_reshape.14
  565.3 58.9 %while.27 = (s32[]{:T(128)}, f32[160,2,3,128]{3,0,2,1:T(8,128)S(1)}, f32[160,2,3]{0,2,1:T(4,128)S(1)}, bf16[20,256,2,128]{3,2,1,0:T(2,128)(2,1)}, bf16[20,256,2,...) while((s32[]{:T(128)}, ...), condition=%wide.region_11.12_spmd.clone, body=%wide.region_9.11_spmd.clone.sunk | while | flops 126813120 | bytes 3013732 | solution.py:82
  566.4 1.4 fusion.60
  575.3 1.4 fusion.60
  590.0 1.4 fusion.60
  595.9 1.4 fusion.60
  610.6 1.4 fusion.60
  616.5 1.4 fusion.60
  624.8 2.7 fusion.12
  (217 shorter events, 112.2 us)
Async XLA Ops:
  7.2 124.2 %all-gather.17.cloned.1.call-start = ((), (), s32[]{:S(2)}) async-start(), calls=%async_computation.6 | async-start | bytes 5263360 | tf_op jit(solution)/shard_map/all_gather | solution.py:23
  7.9 248.1 %all-gather.11.cloned.1.call-start = ((), (), s32[]{:S(2)}) async-start(), calls=%async_computation.3 | async-start | bytes 2703360 | tf_op jit(solution)/shard_map/all_gather | solution.py:70
  14.9 123.7 %copy-start = (bf16[1,160,1536]{2,1,0:T(8,128)(2,1)S(1)}, bf16[1,160,1536]{2,1,0:T(8,128)(2,1)}, u32[]{:S(2)}) copy-start(bf16[1,160,1536]{2,1,0:T(8,128)(2,1)} %param.12) | copy-start | bytes 1474564
  138.6 5.0 copy-start.5
  141.6 4.0 copy-start.2
  142.9 143.8 %all-gather.9.cloned.1.call-start = ((), (), s32[]{:S(2)}) async-start(), calls=%async_computation.2 | async-start | bytes 2703360 | tf_op jit(solution)/shard_map/all_gather | solution.py:71
  145.6 98.4 %all-to-all-start = ((bf16[256,6,768]{2,1,0:T(8,128)(2,1)}), bf16[256,6,768]{2,1,0:T(8,128)(2,1)}, u32[]{:S(2)}, u32[]{:S(2)}) async-start(bf16[256,6,768]{2,1,0:T(8,128)(2,1)} %stack.4), calls=%async_computation | async-start | bytes 6291456 | tf_op jit(solution)/shard_map/all_to_all | solution.py:25
  155.2 250.6 %all-gather.19.cloned.1.call-start = ((), (), s32[]{:S(2)}) async-start(), calls=%async_computation.7 | async-start | bytes 5263360 | tf_op jit(solution)/shard_map/all_gather | solution.py:23
  155.8 375.4 %all-gather.15.cloned.1.call-start = ((), (), s32[]{:S(2)}) async-start(), calls=%async_computation.5 | async-start | bytes 2703360 | tf_op jit(solution)/shard_map/all_gather | solution.py:70
  353.2 59.9 %copy-start.4 = (bf16[160,1536]{1,0:T(8,128)(2,1)}, bf16[160,1536]{1,0:T(8,128)(2,1)S(1)}, u32[]{:S(2)}) copy-start(bf16[160,1536]{1,0:T(8,128)(2,1)S(1)} %fusion.11) | copy-start | bytes 1474564
  353.2 59.9 %collective-permute-start = (bf16[160,1536]{1,0:T(8,128)(2,1)S(1)}, bf16[160,1536]{1,0:T(8,128)(2,1)S(1)}, u32[]{:S(2)}, u32[]{:S(2)}) collective-permute-start(bf16[160,1536]{1,0:T(8,128)(2,1)S(1)} %fusion.11), channel_id=1, source_target_pairs={{0,32},{32,64},{64,96},{96,128},{128,160},{160,192},{192,224},{224... | collective-permute-start | bytes 1474568 | tf_op jit(solution)/shard_map/ppermute | solution.py:13
  413.1 3.2 copy-start.1
  413.3 4.3 copy-start.6
  416.3 13.0 %copy-start.3 = (f32[160,1280]{1,0:T(8,128)}, f32[160,1280]{1,0:T(8,128)S(1)}, u32[]{:S(2)}) copy-start(f32[160,1280]{1,0:T(8,128)S(1)} %fusion.21) | copy-start | bytes 2457604
  419.5 99.6 %all-to-all-start.1 = ((bf16[256,6,768]{2,1,0:T(8,128)(2,1)}), bf16[256,6,768]{2,1,0:T(8,128)(2,1)}, u32[]{:S(2)}, u32[]{:S(2)}) async-start(bf16[256,6,768]{2,1,0:T(8,128)(2,1)} %stack.5), calls=%async_computation.1 | async-start | bytes 6291456 | tf_op jit(solution)/shard_map/all_to_all | solution.py:25
  429.1 131.3 %all-gather.13.cloned.1.call-start = ((), (), s32[]{:S(2)}) async-start(), calls=%async_computation.4 | async-start | bytes 2703360 | tf_op jit(solution)/shard_map/all_gather | solution.py:71
Sparse Core Ops, SparseCore 0:
  11.6 119.7 all-gather.16
  143.1 74.0 all-gather.10
  219.6 67.1 all-gather.8
  290.2 115.5 all-gather.18
  417.7 73.6 all-gather.14
  493.1 67.2 all-gather.12
